TPU v7x, 32 devices: a whole 2x2x4 slice. The times are simulated.
32 devices in a mesh: groups: 2 (over y), ctx: 16 (over z, x, core).
Axes of the slice: x: 2, y: 2, z: 4, core: 2. Of those that a mesh axis runs over, the one named last changes fastest.
Arguments:
- queries: bfloat16 [12288, 1024], P(('groups', 'ctx')), parts along dimension 0, may hold values from -14 to 14
- inputs: bfloat16 [12288, 1024], P(('groups', 'ctx')), parts along dimension 0, may hold values from -6 to 6
- w_kv: bfloat16 [1024, 2048], replicated, may hold values from -1 to 1
- rand_blocks: int32 [192, 3], P('groups'), parts along dimension 0, may hold values from 1 to 94, as said below
- w_cross: bfloat16 [1024, 2048], replicated, may hold values from -1 to 1
- vocab_table: bfloat16 [6144, 1024], P('ctx'), may hold values from -14 to 14
- summary_ids: int32 [512], P('groups'), parts along dimension 0, may hold values from 0 to 6143
Outputs:
- attended: bfloat16 [12288, 1024], P(('groups', 'ctx')), parts along dimension 0
- summary: bfloat16 [512, 1024], P(('groups', 'ctx')), parts along dimension 0
There are 2 independent parts, one for each index of `groups`. A program takes and returns all parts, laid end to end along the dimension named above; an argument that names none is the same for every part. Nothing has to cross between parts.
Inputs may be any that keep to these rules, and one draw needn't show every extreme that they name: `rand_blocks`: take each run of 6 query blocks that starts at a multiple of 6: its 18 random blocks never lie in its own run (they may lie in any other run, and may repeat a block of the window), the 3 blocks of one query block lie in different runs, at most 2 of them lie in any one other run and some run holds exactly 2 of them. No random block is block 0 or block 95.
All inputs are finite; a program needn't handle non-finite values.
Results may differ from a plain program's by a relative error of at most 0.0075.
Values may be sent and summed in bfloat16 or wider, within the bound.
A program may use at most 192 MiB of HBM per device.

v0:
```python
import jax
import jax.numpy as jnp
from jax import lax
from jax.sharding import PartitionSpec as P

HEADS = 16
HEAD = 64
BLOCK = 64


MASKED_SCORE = -1e30


def from_root(block, axis, holder):
    block = jnp.where(lax.axis_index(axis) == holder, block, jnp.zeros_like(block))
    return lax.psum(block, axis)


def padded_2(x, sides, width):
    for axis, dim in sides:
        size, length = (lax.axis_size(axis), x.shape[dim])
        up = [(i, (i + 1) % size) for i in range(size - 1)]
        down = [(j, i) for i, j in up]
        last = lax.slice_in_dim(x, length - width, length, axis=dim)
        initial = lax.slice_in_dim(x, 0, width, axis=dim)
        before = lax.ppermute(last, axis, up)
        after = lax.ppermute(initial, axis, down)
        x = jnp.concatenate([before, x, after], axis=dim)
    return x


def partial_rows(query_rows, key_rows, value_rows):
    row_count = query_rows.shape[0]
    key_count = key_rows.shape[0]
    scores = jnp.einsum(
        "qhe,khe->qhk",
        query_rows.reshape(row_count, HEADS, HEAD),
        key_rows.reshape(key_count, HEADS, HEAD),
        preferred_element_type=jnp.float32,
    ) * HEAD ** (-0.5)
    peak = jnp.max(scores, axis=2)
    weights = jnp.exp(scores - peak[:, :, None])
    totals = jnp.sum(weights, axis=2)
    sums = jnp.einsum(
        "qhk,khe->qhe",
        weights,
        value_rows.reshape(key_count, HEADS, HEAD).astype(jnp.float32),
        precision=lax.Precision.HIGHEST,
    )
    return (peak, totals, sums.reshape(row_count, HEADS * HEAD))


def rescale(sums, scaling):
    row_count = sums.shape[0]
    return (sums.reshape(row_count, HEADS, HEAD) * scaling[:, :, None]).reshape(
        row_count, HEADS * HEAD
    )


def normalize(totals, sums):
    row_count = sums.shape[0]
    return (sums.reshape(row_count, HEADS, HEAD) / totals[:, :, None]).reshape(
        row_count, HEADS * HEAD
    )


def global_block(queries, key_value, root, start):
    query_piece = lax.slice_in_dim(queries, start, start + BLOCK, axis=0)
    pair_piece = lax.slice_in_dim(key_value, start, start + BLOCK, axis=0)
    return (from_root(query_piece, "ctx", root), from_root(pair_piece, "ctx", root))


def local(queries, inputs, w_kv, rand_blocks, w_cross, vocab_table, summary_ids):
    devices = lax.axis_size("ctx")
    position = lax.axis_index("ctx")
    row_count, feature_count = inputs.shape
    block_count = row_count // BLOCK
    pick_count = rand_blocks.shape[1]
    total_blocks = block_count * devices
    key_value = jnp.dot(inputs, w_kv, preferred_element_type=jnp.float32).astype(jnp.bfloat16)
    padded_inputs = padded_2(inputs, (("ctx", 0),), BLOCK)
    rim_rows = jnp.concatenate([padded_inputs[:BLOCK], padded_inputs[row_count + BLOCK :]], axis=0)
    rim_pairs = jnp.dot(rim_rows, w_kv, preferred_element_type=jnp.float32).astype(jnp.bfloat16)
    padded = jnp.concatenate([rim_pairs[:BLOCK], key_value, rim_pairs[BLOCK:]], axis=0)
    first_query, first_pair = global_block(queries, key_value, 0, 0)
    last_query, last_pair = global_block(queries, key_value, devices - 1, row_count - BLOCK)
    request_count = pick_count * block_count
    slot_count = (request_count + devices - 2) // (devices - 1)
    requests = rand_blocks.reshape(devices, request_count)
    owners = requests // block_count
    within = requests % block_count
    order = jnp.arange(request_count, dtype=jnp.int32)
    earlier = order[None, :] < order[:, None]
    matching = owners[:, :, None] == owners[:, None, :]
    ranks = jnp.sum(jnp.logical_and(matching, earlier[None, :, :]), axis=2)
    slot_ids = jnp.arange(slot_count, dtype=jnp.int32)
    served = jnp.logical_and(
        (owners == position)[:, None, :], ranks[:, None, :] == slot_ids[None, :, None]
    )
    sources = jnp.sum(jnp.where(served, within[:, None, :], 0), axis=2)
    filled = jnp.any(served, axis=2)
    outgoing = inputs.reshape(block_count, BLOCK, feature_count)[sources]
    outgoing = jnp.where(filled[:, :, None, None], outgoing, jnp.zeros((), jnp.bfloat16))
    arrived = lax.all_to_all(outgoing, "ctx", split_axis=0, concat_axis=0, tiled=True)
    my_owners = lax.dynamic_index_in_dim(owners, position, 0, keepdims=False)
    my_ranks = lax.dynamic_index_in_dim(ranks, position, 0, keepdims=False)
    fetched = arrived.reshape(devices * slot_count, BLOCK, feature_count)[
        my_owners * slot_count + my_ranks
    ]
    far_pairs = jnp.dot(
        fetched.reshape(request_count * BLOCK, feature_count),
        w_kv,
        preferred_element_type=jnp.float32,
    ).astype(jnp.bfloat16)
    far_pairs = far_pairs.reshape(block_count, pick_count * BLOCK, 2 * feature_count)
    framed = padded.reshape(block_count + 2, BLOCK, 2 * feature_count)
    window = jnp.concatenate(
        [framed[:block_count], framed[1 : block_count + 1], framed[2:]], axis=1
    )
    end_pairs = jnp.concatenate([first_pair, last_pair], axis=0)
    end_pairs = jnp.broadcast_to(end_pairs[None], (block_count, 2 * BLOCK, 2 * feature_count))
    key_sets = jnp.concatenate([window, end_pairs, far_pairs], axis=1)
    span = key_sets.shape[1]
    numbers = position * block_count + jnp.arange(block_count, dtype=jnp.int32)
    flags = jnp.stack(
        [numbers >= 2, jnp.ones((block_count,), dtype=bool), numbers <= total_blocks - 3], axis=1
    )
    valid = jnp.concatenate(
        [jnp.repeat(flags, BLOCK, axis=1), jnp.ones((block_count, span - 3 * BLOCK), dtype=bool)],
        axis=1,
    )
    query_blocks = queries.reshape(block_count, BLOCK, HEADS, HEAD)
    key_blocks = key_sets[:, :, :feature_count].reshape(block_count, span, HEADS, HEAD)
    value_blocks = key_sets[:, :, feature_count:].reshape(block_count, span, HEADS, HEAD)
    scores = jnp.einsum(
        "bqhe,bkhe->bhqk", query_blocks, key_blocks, preferred_element_type=jnp.float32
    ) * HEAD ** (-0.5)
    scores = jnp.where(valid[:, None, None, :], scores, MASKED_SCORE)
    weights = jnp.exp(scores - jnp.max(scores, axis=3, keepdims=True))
    probs = (weights / jnp.sum(weights, axis=3, keepdims=True)).astype(jnp.bfloat16)
    sparse_out = jnp.einsum(
        "bhqk,bkhe->bqhe", probs, value_blocks, preferred_element_type=jnp.float32
    )
    sparse_out = sparse_out.reshape(block_count, BLOCK, feature_count)
    end_queries = jnp.concatenate([first_query, last_query], axis=0)
    end_peak, end_totals, end_sums = partial_rows(
        end_queries, key_value[:, :feature_count], key_value[:, feature_count:]
    )
    shard_rows = vocab_table.shape[0]
    offsets = summary_ids - position * shard_rows
    inside = jnp.logical_and(offsets >= 0, offsets < shard_rows)
    looked = vocab_table[jnp.clip(offsets, 0, shard_rows - 1)].astype(jnp.float32)
    looked = jnp.where(inside[:, None], looked, 0.0)
    end_top = lax.pmax(end_peak, "ctx")
    end_scale = jnp.exp(end_peak - end_top)
    global_sums, global_totals, gathered_rows = lax.psum(
        (rescale(end_sums, end_scale), end_totals * end_scale, looked), "ctx"
    )
    global_out = normalize(global_totals, global_sums)
    sparse_out = sparse_out.at[0].set(jnp.where(position == 0, global_out[:BLOCK], sparse_out[0]))
    sparse_out = sparse_out.at[block_count - 1].set(
        jnp.where(position == devices - 1, global_out[BLOCK:], sparse_out[block_count - 1])
    )
    attended = sparse_out.reshape(row_count, feature_count).astype(jnp.bfloat16)
    encoded = (inputs.astype(jnp.float32) + attended.astype(jnp.float32)).astype(jnp.bfloat16)
    cross = jnp.dot(encoded, w_cross, preferred_element_type=jnp.float32).astype(jnp.bfloat16)
    summary_queries = gathered_rows.astype(jnp.bfloat16)
    cross_peak, cross_totals, cross_sums = partial_rows(
        summary_queries, cross[:, :feature_count], cross[:, feature_count:]
    )
    share = summary_queries.shape[0] // devices
    top_scores = lax.pmax(cross_peak, "ctx")
    scaling = jnp.exp(cross_peak - top_scores)
    scaled_sums = rescale(cross_sums, scaling)
    whole_sums, whole_totals = lax.psum((scaled_sums, cross_totals * scaling), "ctx")
    summary = lax.dynamic_slice_in_dim(
        normalize(whole_totals, whole_sums), position * share, share, 0
    )
    return (attended, summary.astype(jnp.bfloat16))


def solution(mesh):
    return jax.shard_map(
        local,
        mesh=mesh,
        in_specs=(
            P(("groups", "ctx"), None),
            P(("groups", "ctx"), None),
            P(),
            P("groups", None),
            P(),
            P("ctx", None),
            P("groups"),
        ),
        out_specs=(P(("groups", "ctx"), None), P(("groups", "ctx"), None)),
        check_vma=False,
    )
```

profile of v0, /device:TPU:11, one launch (start us, length us, event | category | flops | bytes accessed | tf_op | source)
XLA Modules:
  0.0 554.6 jit_solution(12927445662915458482)
XLA Ops:
  10.4 3.9 gather_fusion
  14.3 4.5 broadcast_select_fusion
  18.8 6.7 %all-to-all-start = ((bf16[16,2,64,1024]{3,2,1,0:T(8,128)(2,1)}), bf16[16,2,64,1024]{3,2,1,0:T(8,128)(2,1)}, u32[]{:S(2)}, u32[]{:S(2)}) async-start(bf16[16,2,64,1024]{3,2,1,0:T(8,128)(2,1)} %broadcast_select_fusion), calls=%async_computation | async-start | bytes 8388608 | tf_op jit(solution)/shard_map/all_to_all | solution.py:104
  26.2 3.3 collective-permute-start
  33.1 4.0 convolution_convert_fusion.2
  53.4 69.3 %collective-permute-done = bf16[64,1024]{1,0:T(8,128)(2,1)S(1)} collective-permute-done((bf16[64,1024]{1,0:T(8,128)(2,1)}, bf16[64,1024]{1,0:T(8,128)(2,1)S(1)}, u32[]{:S(2)}, u32[]{:S(2)}) %collective-permute-start) | collective-permute-done | bytes 131104 | tf_op jit(solution)/shard_map/ppermute | solution.py:26
  131.7 49.2 %all-reduce.12.cloned.1.call-done = (bf16[64,2048]{1,0:T(8,128)(2,1)}, bf16[64,2048]{1,0:T(8,128)(2,1)}, bf16[64,1024]{1,0:T(8,128)(2,1)}, bf16[64,1024]{1,0:T(8,128)(2,1)}) async-done(((bf16[64,2048]{1,0:T(8,128)(2,1)}, bf16[64,2048]{1,0:T(8,128)(2,1)}, bf16[64,1024]{1,0:T(8,128)(2,1)}, bf16[64,1024]{1,0:T(8,128)(2,1)}), (bf16[64,2048]{1,0:T(8,128)(2,1)}, bf16[64,2048]{1,0:T(8,128)(2,1)}, ...) | async-done | bytes 786448 | tf_op jit(solution)/shard_map/psum | solution.py:16
  184.4 22.7 %pmax.14 = f32[128,16]{0,1:T(8,128)S(1)} all-reduce(f32[128,16]{0,1:T(8,128)S(1)} %get-tuple-element.68), channel_id=1, replica_groups=mesh['groups'=2,'ctx'=16] {'ctx'}, use_global_device_ids=true, to_apply=%region_10.11 | all-reduce | flops 2048 | bytes 16384 | tf_op jit(solution)/shard_map/pmax | solution.py:154
  215.7 64.7 %all-reduce.13 = (f32[128,16]{0,1:T(8,128)S(1)}, bf16[256,1024]{1,0:T(8,128)(2,1)S(1)}) all-reduce(f32[128,16]{0,1:T(8,128)S(1)} %get-tuple-element.42, f32[256,1024]{1,0:T(8,128)S(1)} %copy-done.4), channel_id=1, replica_groups=mesh['groups'=2,'ctx'=16] {'ctx'}, use_global_device_ids=true, to_apply=%region_13.14 | all-reduce | flops 264192 | bytes 1589248 | tf_op jit(solution)/shard_map/psum | solution.py:156
  281.4 29.3 %all-reduce.8.cloned.1.call-done = f32[128,16,64]{0,2,1:T(8,128)} async-done(((f32[128,16,64]{0,2,1:T(8,128)}), f32[128,16,64]{0,2,1:T(8,128)}) %all-reduce.8.cloned.1.call-update) | async-done | bytes 524304 | tf_op jit(solution)/shard_map/psum | solution.py:156
  312.9 4.5 gather_fusion.1
  317.4 7.6 %convolution_convert_fusion = bf16[1152,2048]{1,0:T(8,128)(2,1)S(1)} fusion(bf16[1152,1024]{1,0:T(8,128)(2,1)} %bitcast.106, bf16[1024,2048]{1,0:T(8,128)(2,1)} %param.13), kind=kOutput, calls=%fused_computation.10 | convolution fusion | flops 4834197504 | bytes 11272192 | tf_op jit(solution)/shard_map/dot_general | solution.py:110
  327.5 10.4 %fusion.61 = (bf16[6,512,1024]{2,1,0:T(8,128)(2,1)}, bf16[6,512,1024]{2,1,0:T(8,128)(2,1)}) fusion(bf16[6,512,2048]{2,1,0:T(8,128)(2,1)} %constant_dynamic-update-slice_fusion), kind=kLoop, calls=%fused_computation.103 | loop fusion | bytes 25165824 | tf_op jit(solution)/shard_map/slice | solution.py:133
  337.9 8.7 %copy.108 = bf16[6,512,1024]{1,2,0:T(8,128)(2,1)} copy(bf16[6,512,1024]{2,1,0:T(8,128)(2,1)} %get-tuple-element.46) | data formatting | bytes 12582912 | tf_op jit(solution)/shard_map/slice | solution.py:133
  346.6 8.8 %copy.107 = bf16[6,512,1024]{1,2,0:T(8,128)(2,1)} copy(bf16[6,512,1024]{2,1,0:T(8,128)(2,1)} %get-tuple-element.47) | data formatting | bytes 12582912 | tf_op jit(solution)/shard_map/slice | solution.py:134
  355.4 11.1 %fusion.67 = (f32[6,16,64]{2,1,0:T(8,128)S(1)}, f32[6,16,64,512]{3,2,1,0:T(8,128)}) fusion(pred[6,512]{1,0:T(8,128)(4,1)S(1)} %concatenate.31, bf16[6,512,16,64]{1,3,2,0:T(8,128)(2,1)} %bitcast.95, bf16[6,64,16,64]{3,2,1,0:T(8,128)(2,1)S(1)} %copy-done.7), kind=kOutput, calls=%fused_computation.109 | convolution fusion | flops 415236608 | bytes 19688448 | tf_op jit(solution)/shard_map/sub | solution.py:139
  366.4 8.3 %fusion.8 = bf16[6,16,64,64]{3,2,1,0:T(8,128)(2,1)S(1)} fusion(bf16[6,512,16,64]{1,3,2,0:T(8,128)(2,1)} %bitcast.96, f32[6,16,64,512]{3,2,1,0:T(8,128)} %get-tuple-element.67, f32[6,16,64]{2,1,0:T(8,128)S(1)} %get-tuple-element.66), kind=kOutput, calls=%fused_computation.16 | convolution fusion | flops 408944640 | bytes 19685376 | tf_op jit(solution)/shard_map/bhqk,bkhe->bqhe/dot_general | solution.py:141
  375.9 4.3 convolution_convert_fusion.1
  381.2 3.7 bitcast_reduce_fusion.1
  384.9 45.1 %pmax.15 = f32[256,16]{0,1:T(8,128)S(1)} all-reduce(f32[256,16]{0,1:T(8,128)S(1)} %get-tuple-element.70), channel_id=1, replica_groups=mesh['groups'=2,'ctx'=16] {'ctx'}, use_global_device_ids=true, to_apply=%region_16.17 | all-reduce | flops 4096 | bytes 32768 | tf_op jit(solution)/shard_map/pmax | solution.py:172
  430.1 3.8 fusion.10
  434.3 7.2 %fusion.33 = f32[256,16,64]{0,2,1:T(8,128)} fusion(bf16[384,16,64]{0,2,1:T(8,128)(2,1)S(1)} %bitcast.104, f32[16,384,256]{2,1,0:T(8,128)} %get-tuple-element.71, f32[256,16]{0,1:T(8,128)S(1)} %get-tuple-element.70, f32[256,16]{0,1:T(8,128)S(1)} %get-tuple-element.41), kind=kOutput, calls=%fused_computation.42 | convolution fusion | flops 1211367424 | bytes 8159232 | tf_op jit(solution)/shard_map/qhk,khe->qhe/dot_general | solution.py:44
  441.5 59.7 %psum.71 = f32[256,16]{0,1:T(8,128)S(1)} all-reduce(f32[256,16]{0,1:T(8,128)S(1)} %get-tuple-element.40), channel_id=1, replica_groups=mesh['groups'=2,'ctx'=16] {'ctx'}, use_global_device_ids=true, to_apply=%region_19.20 | all-reduce | flops 4096 | bytes 32768 | tf_op jit(solution)/shard_map/psum | solution.py:175
  501.2 44.6 %all-reduce.10.cloned.1.call-done = f32[256,1024]{0,1:T(8,128)} async-done(((f32[256,1024]{0,1:T(8,128)}), f32[256,1024]{0,1:T(8,128)}) %all-reduce.10.cloned.1.call-update) | async-done | bytes 1048592 | tf_op jit(solution)/shard_map/psum | solution.py:175
  (106 shorter events, 55.3 us)
Async XLA Ops:
  7.2 32.2 %copy-start = (bf16[384,1024]{1,0:T(8,128)(2,1)S(1)}, bf16[384,1024]{1,0:T(8,128)(2,1)}, u32[]{:S(2)}) copy-start(bf16[384,1024]{1,0:T(8,128)(2,1)} %param.16) | copy-start | bytes 2359300
  18.8 6.7 %copy-start.3 = (bf16[384,1024]{1,0:T(8,128)(2,1)S(1)}, bf16[384,1024]{1,0:T(8,128)(2,1)}, u32[]{:S(2)}) copy-start(bf16[384,1024]{1,0:T(8,128)(2,1)} %param.12) | copy-start | bytes 2359300
  18.8 294.1 %all-to-all-start = ((bf16[16,2,64,1024]{3,2,1,0:T(8,128)(2,1)}), bf16[16,2,64,1024]{3,2,1,0:T(8,128)(2,1)}, u32[]{:S(2)}, u32[]{:S(2)}) async-start(bf16[16,2,64,1024]{3,2,1,0:T(8,128)(2,1)} %broadcast_select_fusion), calls=%async_computation | async-start | bytes 8388608 | tf_op jit(solution)/shard_map/all_to_all | solution.py:104
  25.5 155.4 %all-reduce.12.cloned.1.call-start = ((), (), s32[]{:S(2)}) async-start(), calls=%async_computation.3 | async-start | bytes 1572864 | tf_op jit(solution)/shard_map/psum | solution.py:16
  26.2 96.5 %collective-permute-start = (bf16[64,1024]{1,0:T(8,128)(2,1)}, bf16[64,1024]{1,0:T(8,128)(2,1)S(1)}, u32[]{:S(2)}, u32[]{:S(2)}) collective-permute-start(bf16[64,1024]{1,0:T(8,128)(2,1)} %get-tuple-element.58), channel_id=1, source_target_pairs={{0,1},{1,2},{2,3},{3,4},{4,5},{5,6},{6,7},{7,8},{8,9},{9,10},{10,1... | collective-permute-start | bytes 393224 | tf_op jit(solution)/shard_map/ppermute | solution.py:26
  29.5 94.8 %collective-permute-start.1 = (bf16[64,1024]{1,0:T(8,128)(2,1)S(1)}, bf16[64,1024]{1,0:T(8,128)(2,1)S(1)}, u32[]{:S(2)}, u32[]{:S(2)}) collective-permute-start(bf16[64,1024]{1,0:T(8,128)(2,1)S(1)} %get-tuple-element.59), channel_id=1, source_target_pairs={{1,0},{2,1},{3,2},{4,3},{5,4},{6,5},{7,6},{8,7},{9,8},{10,9},{11,1... | collective-permute-start | bytes 393224 | tf_op jit(solution)/shard_map/ppermute | solution.py:27
  38.0 272.7 %all-reduce.8.cloned.1.call-start = ((), (), s32[]{:S(2)}) async-start(), calls=%async_computation.1 | async-start | bytes 1048576 | tf_op jit(solution)/shard_map/psum | solution.py:156
  41.4 5.5 copy-start.8
  46.9 6.5 %copy-start.11 = (s32[18]{0:T(128)S(1)}, s32[18]{0:T(128)}, u32[]{:S(2)}) copy-start(s32[18]{0:T(128)} %fusion.53) | copy-start | bytes 220
  180.9 28.9 %copy-start.5 = (bf16[384,1024]{0,1:T(8,128)(2,1)S(1)}, bf16[384,1024]{0,1:T(8,128)(2,1)}, u32[]{:S(2)}) copy-start(bf16[384,1024]{0,1:T(8,128)(2,1)} %copy.111) | copy-start | bytes 2359300
  207.1 2.8 copy-start.2
  207.1 5.4 copy-start.10
  210.0 5.7 %copy-start.4 = (f32[256,1024]{1,0:T(8,128)S(1)}, f32[256,1024]{1,0:T(8,128)}, u32[]{:S(2)}) copy-start(f32[256,1024]{1,0:T(8,128)} %convert_select_fusion) | copy-start | bytes 3145732
  212.5 333.3 %all-reduce.10.cloned.1.call-start = ((), (), s32[]{:S(2)}) async-start(), calls=%async_computation.2 | async-start | bytes 2097152 | tf_op jit(solution)/shard_map/psum | solution.py:175
  346.6 8.8 %copy-start.7 = (bf16[6,64,16,64]{3,2,1,0:T(8,128)(2,1)S(1)}, bf16[6,64,16,64]{3,2,1,0:T(8,128)(2,1)}, u32[]{:S(2)}) copy-start(bf16[6,64,16,64]{3,2,1,0:T(8,128)(2,1)} %reshape.293) | copy-start | bytes 2359300
  375.9 4.3 copy-start.9
  380.2 1.0 copy-start.6
  434.3 113.7 %copy-start.1 = (bf16[384,1024]{1,0:T(8,128)(2,1)S(1)}, bf16[384,1024]{1,0:T(8,128)(2,1)}, u32[]{:S(2)}) copy-start(bf16[384,1024]{1,0:T(8,128)(2,1)} %param.16) | copy-start | bytes 2359300
Sparse Core Ops, SparseCore 0:
  38.1 142.7 all-reduce.11
  212.6 98.0 all-reduce.7
  441.6 104.1 all-reduce.9
where the time goes:
time: 560 us; the launch traced here: 555 us
  waiting for transfers between devices  194 us (35%)
  blocking collectives  192 us (34%)
  local copies, waits for them, and re-layouts  62.3 us (11%)
  matrix products  53.8 us (10%)
  other arithmetic  26 us (5%)
  between operations  14.2 us (3%)
  starting transfers between devices  12.1 us (2%)
    ppermute x1, waiting for transfers between devices, padded_2(): before = lax.ppermute(last, axis, up)  69.3 us
    psum x1, blocking collectives, local(): lax.psum((rescale(end_sums, end_scale), end_totals * end_scale, looked),...  64.7 us
    psum x1, blocking collectives, local(): lax.psum((scaled_sums, cross_totals * scaling), 'ctx')  59.7 us
    psum x1, waiting for transfers between devices, from_root(): return lax.psum(block, axis)  49.2 us
    pmax x1, blocking collectives, local(): top_scores = lax.pmax(cross_peak, 'ctx')  45.1 us
    psum x1, waiting for transfers between devices, local(): lax.psum((scaled_sums, cross_totals * scaling), 'ctx')  44.6 us
    psum x1, waiting for transfers between devices, local(): lax.psum((rescale(end_sums, end_scale), end_totals * end_scale, looked),...  29.3 us
    pmax x1, blocking collectives, local(): end_top = lax.pmax(end_peak, 'ctx')  22.7 us
  transfers between devices with their start and end apart: 6, of which 5 were waited for; matrix products, arithmetic and copies ran while one was open for 8% of the time, Pallas kernels for 0%

commit v1 on v0

v1 whole, which is shorter than its diff:
```python
import functools

import jax
import jax.numpy as jnp
from jax import lax
from jax.experimental import pallas as pl
from jax.experimental.pallas import tpu as pltpu
from jax.sharding import PartitionSpec as P

HEADS = 16
HEAD = 64
BLOCK = 64
LANES = 128
PAIRS = HEADS // 2
MASKED_SCORE = -1e30
MESH = pl.DeviceIdType.MESH
VMEM = pl.BlockSpec(memory_space=pltpu.VMEM)
ANY = pl.BlockSpec(memory_space=pl.ANY)
SMEM = pl.BlockSpec(memory_space=pltpu.SMEM)
VMEM_LIMIT = 48 * 1024 * 1024


def exchange_kernel(n, count, same, *refs):
    sources = refs[:count]
    targets = refs[count : 2 * count]
    send_sem, recv_sem, own_sem = refs[2 * count :]
    me = lax.axis_index("ctx")

    def piece(ref, peer):
        return ref if same else ref.at[peer]

    barrier = pltpu.get_barrier_semaphore()

    def greet(k, carry):
        peer = lax.rem(me + k, n)
        pl.semaphore_signal(barrier, inc=1, device_id={"ctx": peer}, device_id_type=MESH)
        return carry

    lax.fori_loop(1, n, greet, 0)
    own = [
        pltpu.make_async_copy(piece(sources[i], me), targets[i].at[me], own_sem.at[i])
        for i in range(count)
    ]
    for copy in own:
        copy.start()
    pl.semaphore_wait(barrier, n - 1)

    def push(i, peer, slot):
        return pltpu.make_async_remote_copy(
            piece(sources[i], peer),
            targets[i].at[slot],
            send_sem.at[i, peer],
            recv_sem.at[i, slot],
            device_id={"ctx": peer},
            device_id_type=MESH,
        )

    def send(k, carry):
        peer = lax.rem(me + k, n)
        for i in range(count):
            push(i, peer, me).start()
        return carry

    lax.fori_loop(1, n, send, 0)

    def finish(k, carry):
        peer = lax.rem(me + n - k, n)
        for i in range(count):
            push(i, peer, peer).wait_recv()
            push(i, peer, peer).wait_send()
        return carry

    lax.fori_loop(1, n, finish, 0)
    for copy in own:
        copy.wait()


def exchange(arrays, collective_id, same=False):
    n = lax.axis_size("ctx")
    count = len(arrays)
    shapes = [((n,) + x.shape) if same else x.shape for x in arrays]
    return pl.pallas_call(
        functools.partial(exchange_kernel, n, count, same),
        out_shape=[jax.ShapeDtypeStruct(s, x.dtype) for s, x in zip(shapes, arrays)],
        in_specs=[ANY] * count,
        out_specs=[ANY] * count,
        scratch_shapes=[
            pltpu.SemaphoreType.DMA((count, n)),
            pltpu.SemaphoreType.DMA((count, n)),
            pltpu.SemaphoreType.DMA((count,)),
        ],
        compiler_params=pltpu.CompilerParams(collective_id=collective_id, has_side_effects=True),
        name=f"exchange_{collective_id}",
    )(*arrays)


def dot_t(a, b):
    return lax.dot_general(a, b, (((1,), (1,)), ((), ())), preferred_element_type=jnp.float32)


def stacked_pair(q):
    q = q * jnp.asarray(HEAD**-0.5, q.dtype)
    left = lax.broadcasted_iota(jnp.int32, q.shape, 1) < HEAD
    zero = jnp.zeros_like(q)
    return jnp.concatenate([jnp.where(left, q, zero), jnp.where(left, zero, q)], axis=0)


def unstacked_pair(o):
    rows = o.shape[0] // 2
    left = lax.broadcasted_iota(jnp.int32, (rows, LANES), 1) < HEAD
    return jnp.where(left, o[:rows], o[rows:])


def project(x_ref, w_ref, out_ref, tile):
    rows, cols = out_ref.shape
    width = 512

    def step(t, carry):
        at = pl.ds(pl.multiple_of(t * tile, tile), tile)
        x = x_ref[at, :]
        for c in range(cols // width):
            y = jnp.dot(
                x, w_ref[:, c * width : (c + 1) * width], preferred_element_type=jnp.float32
            )
            out_ref[at, c * width : (c + 1) * width] = y.astype(out_ref.dtype)
        return carry

    lax.fori_loop(0, rows // tile, step, 0)


def partial_attention(q_ref, kv_ref, out_ref, log_ref):
    rows, features = q_ref.shape
    place = lax.broadcasted_iota(jnp.int32, (rows, LANES), 1)
    logs = jnp.zeros((rows, LANES), jnp.float32)
    for p in range(PAIRS):
        lanes = slice(p * LANES, (p + 1) * LANES)
        values = slice(features + p * LANES, features + (p + 1) * LANES)
        scores = dot_t(stacked_pair(q_ref[:, lanes]), kv_ref[:, lanes])
        peak = jnp.max(scores, axis=1, keepdims=True)
        weights = jnp.exp(scores - peak)
        totals = jnp.sum(weights, axis=1, keepdims=True)
        sums = jnp.dot(
            weights.astype(jnp.bfloat16), kv_ref[:, values], preferred_element_type=jnp.float32
        )
        out_ref[:, lanes] = unstacked_pair(sums / totals).astype(out_ref.dtype)
        log = peak + jnp.log(totals)
        logs = jnp.where(place == 2 * p, log[:rows], logs)
        logs = jnp.where(place == 2 * p + 1, log[rows:], logs)
    log_ref[...] = logs


def global_kernel(q_ref, x_ref, w_ref, out_ref, log_ref, kv_ref):
    project(x_ref, w_ref, kv_ref, 128)
    partial_attention(q_ref, kv_ref, out_ref, log_ref)


def global_partial(q, x, w):
    return pl.pallas_call(
        global_kernel,
        out_shape=[
            jax.ShapeDtypeStruct(q.shape, jnp.bfloat16),
            jax.ShapeDtypeStruct((q.shape[0], LANES), jnp.float32),
        ],
        in_specs=[VMEM] * 3,
        out_specs=[VMEM] * 2,
        scratch_shapes=[pltpu.VMEM((x.shape[0], w.shape[1]), jnp.bfloat16)],
        compiler_params=pltpu.CompilerParams(vmem_limit_bytes=VMEM_LIMIT),
        cost_estimate=pl.CostEstimate(
            flops=2 * x.size * w.shape[1], bytes_accessed=6 << 20, transcendentals=1 << 20
        ),
        name="global_partial",
    )(q, x, w)


def block_kernel(
    pick_count,
    ids_ref,
    edge_ref,
    all_ref,
    q_ref,
    x_ref,
    w_kv_ref,
    w_cross_ref,
    ends_ref,
    sq_ref,
    attended_ref,
    out_ref,
    log_ref,
    rows_ref,
    kv_ref,
    sem,
):
    row_count, features = x_ref.shape
    block_count = row_count // BLOCK
    slots = rows_ref.shape[0] // BLOCK
    far_start = (block_count + 4) * BLOCK
    span = (5 + pick_count) * BLOCK

    def fetch(i):
        return pltpu.make_async_copy(
            all_ref.at[ids_ref[i]],
            rows_ref.at[pl.ds(pl.multiple_of(i * BLOCK, BLOCK), BLOCK)],
            sem.at[i],
        )

    for i in range(slots):
        fetch(i).start()
    for i in range(slots):
        fetch(i).wait()
    project(rows_ref, w_kv_ref, kv_ref, 2 * BLOCK)

    column = lax.broadcasted_iota(jnp.int32, (2 * BLOCK, span), 1)

    def one_block(b, carry):
        first = edge_ref[0] + b
        hidden = jnp.logical_or(
            jnp.logical_and(column < BLOCK, first < 2),
            jnp.logical_and(
                jnp.logical_and(column >= 2 * BLOCK, column < 3 * BLOCK), first > edge_ref[1] - 3
            ),
        )
        near = pl.ds(pl.multiple_of(b * BLOCK, BLOCK), 3 * BLOCK)
        ends = pl.ds((block_count + 2) * BLOCK, 2 * BLOCK)
        far = pl.ds(
            pl.multiple_of(far_start + b * pick_count * BLOCK, BLOCK), pick_count * BLOCK
        )
        here = pl.ds(pl.multiple_of(b * BLOCK, BLOCK), BLOCK)
        for p in range(PAIRS):
            lanes = slice(p * LANES, (p + 1) * LANES)
            values = slice(features + p * LANES, features + (p + 1) * LANES)
            k = jnp.concatenate(
                [kv_ref[near, lanes], kv_ref[ends, lanes], kv_ref[far, lanes]], axis=0
            )
            v = jnp.concatenate(
                [kv_ref[near, values], kv_ref[ends, values], kv_ref[far, values]], axis=0
            )
            scores = dot_t(stacked_pair(q_ref[here, lanes]), k)
            scores = jnp.where(hidden, MASKED_SCORE, scores)
            weights = jnp.exp(scores - jnp.max(scores, axis=1, keepdims=True))
            totals = jnp.sum(weights, axis=1, keepdims=True)
            probs = (weights * (1.0 / totals)).astype(jnp.bfloat16)
            o = jnp.dot(probs, v, preferred_element_type=jnp.float32)
            attended_ref[here, lanes] = unstacked_pair(o).astype(jnp.bfloat16)
        return carry

    lax.fori_loop(0, block_count, one_block, 0)

    @pl.when(edge_ref[0] == 0)
    def _():
        attended_ref[:BLOCK] = ends_ref[:BLOCK]

    @pl.when(edge_ref[0] + block_count == edge_ref[1])
    def _():
        attended_ref[row_count - BLOCK :] = ends_ref[BLOCK:]

    encoded = x_ref[...].astype(jnp.float32) + attended_ref[...].astype(jnp.float32)
    rows_ref[:row_count] = encoded.astype(jnp.bfloat16)
    project(rows_ref.at[:row_count], w_cross_ref, kv_ref.at[:row_count], 2 * BLOCK)
    partial_attention(sq_ref, kv_ref.at[:row_count], out_ref, log_ref)


def block_attention(ids, edge, everything, q, x, w_kv, w_cross, ends, sq, pick_count):
    slots = ids.shape[0]
    features = x.shape[1]
    return pl.pallas_call(
        functools.partial(block_kernel, pick_count),
        out_shape=[
            jax.ShapeDtypeStruct(q.shape, jnp.bfloat16),
            jax.ShapeDtypeStruct(sq.shape, jnp.bfloat16),
            jax.ShapeDtypeStruct((sq.shape[0], LANES), jnp.float32),
        ],
        in_specs=[SMEM, SMEM, ANY] + [VMEM] * 6,
        out_specs=[VMEM] * 3,
        scratch_shapes=[
            pltpu.VMEM((slots * BLOCK, features), jnp.bfloat16),
            pltpu.VMEM((slots * BLOCK, 2 * features), jnp.bfloat16),
            pltpu.SemaphoreType.DMA((slots,)),
        ],
        compiler_params=pltpu.CompilerParams(vmem_limit_bytes=VMEM_LIMIT),
        cost_estimate=pl.CostEstimate(
            flops=20 << 30, bytes_accessed=16 << 20, transcendentals=5 << 20
        ),
        name="block_attention",
    )(ids, edge, everything, q, x, w_kv, w_cross, ends, sq)


def combined(outs, logs):
    n, rows, features = outs.shape
    logs = logs[:, :, :HEADS]
    weights = jnp.exp(logs - jnp.max(logs, axis=0, keepdims=True))
    weights = weights / jnp.sum(weights, axis=0, keepdims=True)
    spread = jnp.broadcast_to(weights[:, :, :, None], (n, rows, HEADS, HEAD))
    spread = spread.reshape(n, rows, features)
    return jnp.sum(outs.astype(jnp.float32) * spread, axis=0).astype(jnp.bfloat16)


def dealt(x, n, each):
    x = jnp.pad(x, ((0, n * each - x.shape[0]), (0, 0)))
    return x.reshape(n, each, x.shape[1])


def local(queries, inputs, w_kv, rand_blocks, w_cross, vocab_table, summary_ids):
    n = lax.axis_size("ctx")
    position = lax.axis_index("ctx")
    row_count, features = inputs.shape
    block_count = row_count // BLOCK
    pick_count = rand_blocks.shape[1]
    total_blocks = block_count * n
    shard_rows = vocab_table.shape[0]
    summary_count = summary_ids.shape[0]
    share = summary_count // n
    each = -(-BLOCK // n)

    everything = lax.all_gather(inputs, "ctx", axis=0, tiled=True)
    everything = everything.reshape(total_blocks, BLOCK, features)

    offsets = summary_ids - position * shard_rows
    inside = jnp.logical_and(offsets >= 0, offsets < shard_rows)
    looked = vocab_table[jnp.clip(offsets, 0, shard_rows - 1)]
    looked = jnp.where(inside[:, None], looked, jnp.zeros((), looked.dtype))
    message = jnp.concatenate(
        [
            looked.reshape(n, share, features),
            dealt(queries[:BLOCK], n, each),
            dealt(queries[row_count - BLOCK :], n, each),
        ],
        axis=1,
    )
    (received,) = exchange([message], 1)
    mine = jnp.concatenate(
        [
            jnp.sum(received[:, :share].astype(jnp.float32), axis=0).astype(jnp.bfloat16),
            received[0, share : share + each],
            received[n - 1, share + each :],
        ],
        axis=0,
    )
    (rows,) = exchange([mine], 2, same=True)
    summary_queries = rows[:, :share].reshape(summary_count, features)
    first = rows[:, share : share + each].reshape(n * each, features)[:BLOCK]
    last = rows[:, share + each :].reshape(n * each, features)[:BLOCK]
    end_out, end_log = global_partial(jnp.concatenate([first, last], axis=0), inputs, w_kv)

    def split(x):
        return jnp.concatenate([dealt(x[:BLOCK], n, each), dealt(x[BLOCK:], n, each)], axis=1)

    got_out, got_log = exchange([split(end_out), split(end_log)], 3)
    (ends,) = exchange([combined(got_out, got_log)], 4, same=True)
    ends = jnp.concatenate(
        [
            ends[:, :each].reshape(n * each, features)[:BLOCK],
            ends[:, each:].reshape(n * each, features)[:BLOCK],
        ],
        axis=0,
    )

    start = position * block_count
    near = jnp.clip(start - 1 + jnp.arange(block_count + 2, dtype=jnp.int32), 0, total_blocks - 1)
    fixed = jnp.array([0, total_blocks - 1], jnp.int32)
    picks = lax.dynamic_slice_in_dim(rand_blocks, start, block_count, 0).reshape(-1)
    ids = jnp.concatenate([near, fixed, picks.astype(jnp.int32)])
    edge = jnp.stack([start, jnp.full_like(start, total_blocks)]).astype(jnp.int32)
    attended, part, logs = block_attention(
        ids, edge, everything, queries, inputs, w_kv, w_cross, ends, summary_queries, pick_count
    )
    parts, all_logs = exchange(
        [part.reshape(n, share, features), logs.reshape(n, share, LANES)], 5
    )
    return attended, combined(parts, all_logs)


def solution(mesh):
    return jax.shard_map(
        local,
        mesh=mesh,
        in_specs=(
            P(("groups", "ctx"), None),
            P(("groups", "ctx"), None),
            P(),
            P("groups", None),
            P(),
            P("ctx", None),
            P("groups"),
        ),
        out_specs=(P(("groups", "ctx"), None), P(("groups", "ctx"), None)),
        check_vma=False,
    )
```

time: 560 us -> 220 us (0.39)
  blocking collectives: 192 us -> 0 us
  waiting for transfers between devices: 194 us -> 6.77 us
  Pallas kernels: 0 us -> 169 us
  matrix products: 53.8 us -> 0 us
  local copies, waits for them, and re-layouts: 62.3 us -> 14.5 us
  starting transfers between devices: 12.1 us -> 0.04 us
  other arithmetic: 26 us -> 14.5 us
    pallas_call x0 -> x7, Pallas kernels: none -> 169 us  [the longest x5 125 us: exchange(): pl.pallas_call(functools.partial(exchange_kernel, n, count, same), out_sh...]
    psum x2 -> x0, blocking collectives: 124 us -> none  [the longest x1 64.7 us: local(): lax.psum((rescale(end_sums, end_scale), end_totals * end_scale, looked),...]
    psum x3 -> x0, waiting for transfers between devices: 123 us -> none  [the longest x1 49.2 us: from_root(): return lax.psum(block, axis)]
    ppermute x2 -> x0, waiting for transfers between devices: 70.8 us -> none  [the longest x1 69.3 us: padded_2(): before = lax.ppermute(last, axis, up)]
    pmax x2 -> x0, blocking collectives: 67.8 us -> none  [the longest x1 45.1 us: local(): top_scores = lax.pmax(cross_peak, 'ctx')]
    dot_general x9 -> x0, matrix products: 42.7 us -> none  [the longest x2 9.7 us: partial_rows(): jnp.einsum('qhk,khe->qhe', weights, value_rows.reshape(key_count, HEADS,...]
    slice x15 -> x6, local copies, waits for them, and re-layouts: 35.5 us -> 4.64 us  [the longest x1 1.3 us: local(): first = rows[:, share:share + each].reshape(n * each, features)[:BLOCK]]
    sub x1 -> x0, matrix products: 11.1 us -> none  [local(): weights = jnp.exp(scores - jnp.max(scores, axis=3, keepdims=True))]
  transfers between devices with their start and end apart: 6 -> 1, of which waited for: 5 -> 1; matrix products, arithmetic and copies ran while one was open for 8% -> 8% of each run, Pallas kernels for 0% -> 49%
where the time goes in v1:
time: 220 us; the launch traced here: 219 us
  Pallas kernels  169 us (77%)
  local copies, waits for them, and re-layouts  14.5 us (7%)
  other arithmetic  14.5 us (7%)
  between operations  14.3 us (6%)
  waiting for transfers between devices  6.77 us (3%)
    pallas_call x5, Pallas kernels, exchange(): pl.pallas_call(functools.partial(exchange_kernel, n, count, same), out_sh...  125 us
    pallas_call x1, Pallas kernels, block_attention(): pl.pallas_call(functools.partial(block_kernel, pick_count), out_shape=[ja...  39 us
    all_gather x1, waiting for transfers between devices, local(): everything = lax.all_gather(inputs, 'ctx', axis=0, tiled=True)  6.08 us
    pallas_call x1, Pallas kernels, global_partial(): pl.pallas_call(global_kernel, out_shape=[jax.ShapeDtypeStruct(q.shape, jn...  4.68 us
  transfers between devices with their start and end apart: 1, of which 1 were waited for; matrix products, arithmetic and copies ran while one was open for 8% of the time, Pallas kernels for 49%

profile of v1, /device:TPU:11, one launch (start us, length us, event | category | flops | bytes accessed | tf_op | source)
XLA Modules:
  0.0 218.9 jit_solution(8774593349260667238)
XLA Ops:
  8.7 1.0 fusion.5
  9.9 1.2 gather_fusion
  11.2 1.0 pad_maximum_fusion.refs_0_
  12.2 40.6 %exchange_1.1 = bf16[16,24,1024]{2,1,0:T(8,128)(2,1)} custom-call(bf16[16,24,1024]{2,1,0:T(8,128)(2,1)} %pad_maximum_fusion.refs_0_), custom_call_target="tpu_custom_call" | custom-call | tf_op jit(solution)/shard_map/exchange_1/pallas_call | solution.py:82
  52.8 1.1 slice_reduce_fusion
  55.3 21.6 %exchange_2.1 = bf16[16,24,1024]{2,1,0:T(8,128)(2,1)} custom-call(bf16[24,1024]{1,0:T(8,128)(2,1)} %pad_maximum_fusion.5.refs_0_), custom_call_target="tpu_custom_call" | custom-call | tf_op jit(solution)/shard_map/exchange_2/pallas_call | solution.py:82
  76.9 1.2 slice.62
  78.1 1.3 fusion.4
  79.5 2.2 copy-done.5
  81.7 4.7 %global_partial.1 = (bf16[128,1024]{1,0:T(8,128)(2,1)S(1)}, f32[128,128]{1,0:T(8,128)S(1)}) custom-call(bf16[128,1024]{1,0:T(8,128)(2,1)S(1)} %pad_maximum_fusion.1.q_ref, bf16[384,1024]{1,0:T(8,128)(2,1)S(1)} %copy-done.1, bf16[1024,2048]{1,0:T(8,128)(2,1)S(1)} %copy-done.5), custom_call_target="tpu_custom_call" | custom-call | flops 1610612736 | bytes 6291456 | tf_op jit(solution)/shard_map/global_partial/pallas_call | solution.py:158
  88.0 22.2 %exchange_3.1 = (bf16[16,8,1024]{2,1,0:T(8,128)(2,1)}, f32[16,8,128]{2,1,0:T(8,128)}) custom-call(bf16[16,8,1024]{2,1,0:T(8,128)(2,1)} %pad_maximum_fusion.2.refs_0_, f32[16,8,128]{2,1,0:T(8,128)} %pad_maximum_fusion.4.refs_1_), custom_call_target="tpu_custom_call" | custom-call | tf_op jit(solution)/shard_map/exchange_3/pallas_call | solution.py:82
  110.2 0.9 slice_reduce_fusion.2
  113.2 1.1 reshape.79
  114.3 1.8 multiply_reduce_fusion.1.refs_0_
  116.1 17.7 %exchange_4.1 = bf16[16,8,1024]{2,1,0:T(8,128)(2,1)} custom-call(bf16[8,1024]{1,0:T(8,128)(2,1)} %multiply_reduce_fusion.1.refs_0_), custom_call_target="tpu_custom_call" | custom-call | tf_op jit(solution)/shard_map/exchange_4/pallas_call | solution.py:82
  133.8 1.1 fusion.6
  135.5 6.1 %all-gather.2.cloned.1.call-done = bf16[6144,1024]{1,0:T(8,128)(2,1)} async-done(((bf16[384,1024]{1,0:T(8,128)(2,1)}), bf16[6144,1024]{1,0:T(8,128)(2,1)}) %all-gather.2.cloned.1.call-update) | async-done | bytes 12582928 | tf_op jit(solution)/shard_map/all_gather | solution.py:314
  141.6 39.0 %block_attention.1 = (bf16[384,1024]{1,0:T(8,128)(2,1)}, bf16[256,1024]{1,0:T(8,128)(2,1)S(1)}, f32[256,128]{1,0:T(8,128)S(1)}) custom-call(s32[28]{0:T(128)S(1)} %pad_add_fusion.ids_ref, s32[2]{0:T(128)S(1)} %pad_add_fusion.1.edge_ref, bf16[96,64,1024]{2,1,0:T(8,128)(2,1)} %bitcast.22, bf16[384,1024]{1,0:T(8,128)(2,1)S(1)} %copy-done.4, ...), custom_call_target="tpu_custom_call" | custom-call | flops 21474836480 | bytes 16777216 | tf_op jit(solution)/shard_map/block_attention/pallas_call | solution.py:265
  182.1 23.0 %exchange_5.1 = (bf16[16,16,1024]{2,1,0:T(8,128)(2,1)}, f32[16,16,128]{2,1,0:T(8,128)}) custom-call(bf16[16,16,1024]{2,1,0:T(8,128)(2,1)} %bitcast.16, f32[16,16,128]{2,1,0:T(8,128)} %bitcast.18), custom_call_target="tpu_custom_call" | custom-call | tf_op jit(solution)/shard_map/exchange_5/pallas_call | solution.py:82
  205.1 0.9 slice_reduce_fusion.1
  206.0 0.9 fusion.1
  207.0 0.9 fusion
  208.5 1.5 reshape.85
  210.1 2.0 multiply_reduce_fusion
  (53 shorter events, 9.5 us)
Async XLA Ops:
  7.2 2.7 %copy-start = (bf16[384,1024]{1,0:T(8,128)(2,1)S(1)}, bf16[384,1024]{1,0:T(8,128)(2,1)}, u32[]{:S(2)}) copy-start(bf16[384,1024]{1,0:T(8,128)(2,1)} %param.13) | copy-start | bytes 2359300
  7.2 2.6 %copy-start.8 = (s32[256]{0:T(256)S(1)}, s32[256]{0:T(256)}, u32[]{:S(2)}) copy-start(s32[256]{0:T(256)} %param.14) | copy-start | bytes 3076
  7.2 134.4 %all-gather.2.cloned.1.call-start = ((), (), s32[]{:S(2)}) async-start(), calls=%async_computation | async-start | bytes 13369344 | tf_op jit(solution)/shard_map/all_gather | solution.py:314
  55.3 24.2 %copy-start.1 = (bf16[384,1024]{1,0:T(8,128)(2,1)S(1)}, bf16[384,1024]{1,0:T(8,128)(2,1)}, u32[]{:S(2)}) copy-start(bf16[384,1024]{1,0:T(8,128)(2,1)} %x_ref.3) | copy-start | bytes 2359300
  79.5 2.2 %copy-start.5 = (bf16[1024,2048]{1,0:T(8,128)(2,1)S(1)}, bf16[1024,2048]{1,0:T(8,128)(2,1)}, u32[]{:S(2)}) copy-start(bf16[1024,2048]{1,0:T(8,128)(2,1)} %w_kv_ref.1) | copy-start | bytes 12582916
  110.2 4.1 %copy-start.7 = (bf16[16,8,1024]{2,1,0:T(8,128)(2,1)S(1)}, bf16[16,8,1024]{2,1,0:T(8,128)(2,1)}, u32[]{:S(2)}) copy-start(bf16[16,8,1024]{2,1,0:T(8,128)(2,1)} %get-tuple-element.13) | copy-start | bytes 786436
  113.2 21.9 %copy-start.9 = (s32[96,3]{0,1:T(4,128)S(1)}, s32[96,3]{0,1:T(4,128)}, u32[]{:S(2)}) copy-start(s32[96,3]{0,1:T(4,128)} %param.11) | copy-start | bytes 3460
  114.3 27.3 %copy-start.4 = (bf16[384,1024]{1,0:T(8,128)(2,1)S(1)}, bf16[384,1024]{1,0:T(8,128)(2,1)}, u32[]{:S(2)}) copy-start(bf16[384,1024]{1,0:T(8,128)(2,1)} %q_ref.1) | copy-start | bytes 2359300
  180.6 0.8 copy-start.2
  181.4 0.6 copy-start.3
  208.5 1.6 copy-start.6
Sparse Core Ops, SparseCore 0:
  10.3 131.2 all-gather.1

commit v2 on v1

--- a/solution.py
+++ b/solution.py
@@ -20,15 +20,7 @@
 VMEM_LIMIT = 48 * 1024 * 1024
 
 
-def exchange_kernel(n, count, same, *refs):
-    sources = refs[:count]
-    targets = refs[count : 2 * count]
-    send_sem, recv_sem, own_sem = refs[2 * count :]
-    me = lax.axis_index("ctx")
-
-    def piece(ref, peer):
-        return ref if same else ref.at[peer]
-
+def greet_all(me, n):
     barrier = pltpu.get_barrier_semaphore()
 
     def greet(k, carry):
@@ -37,61 +29,379 @@
         return carry
 
     lax.fori_loop(1, n, greet, 0)
+    pl.semaphore_wait(barrier, n - 1)
+
+
+def push(source, target, send_sem, recv_sem, peer):
+    return pltpu.make_async_remote_copy(
+        source, target, send_sem, recv_sem, device_id={"ctx": peer}, device_id_type=MESH
+    )
+
+
+def each_peer(me, n, body):
+    def step(k, carry):
+        body(lax.rem(me + k, n))
+        return carry
+
+    lax.fori_loop(1, n, step, 0)
+
+
+def gather_kernel(
+    n,
+    x_ref,
+    q_ref,
+    looked_ref,
+    all_ref,
+    ends_ref,
+    got_ref,
+    ring_send,
+    ring_recv,
+    side_send,
+    side_recv,
+    got_send,
+    got_recv,
+    ends_send,
+    ends_recv,
+    own_sem,
+):
+    me = lax.axis_index("ctx")
+    chips = n // 2
+    half = chips // 2
+    core = me % 2
+    chip = me // 2
+    odd = chip % 2
+    place = (1 - odd) * (chip // 2) + odd * (chips - 1 - chip // 2)
+    sibling = me + 1 - 2 * core
+    row_count = q_ref.shape[0]
+
+    def device(at, on_core):
+        at = (at + chips) % chips
+        back = at // half
+        return 2 * ((1 - back) * 2 * at + back * (2 * (chips - 1 - at) + 1)) + on_core
+
+    streams = [(d, h) for h in range(2) for d in range(2)]
+
+    def hops(d, h):
+        return half if d == h else half - 1
+
+    def ring(d, h, s):
+        sign = 1 - 2 * d
+        owner = device(place - sign * s, core)
+        source = x_ref.at[h] if s == 0 else all_ref.at[owner, h]
+        return push(
+            source,
+            all_ref.at[owner, h],
+            ring_send.at[d, h, s],
+            ring_recv.at[d, h, s],
+            device(place + sign, core),
+        )
+
+    def arrival(d, h, s):
+        owner = device(place - (1 - 2 * d) * (s + 1), core)
+        landed = all_ref.at[owner, h]
+        return push(landed, landed, ring_send.at[d, h, s], ring_recv.at[d, h, s], sibling)
+
+    def side(d, h, s, on_core):
+        owner = device(place - (1 - 2 * d) * s, on_core)
+        source = all_ref.at[owner, h]
+        if s == 0:
+            source = x_ref.at[h]
+        return push(
+            source, all_ref.at[owner, h], side_send.at[d, h, s], side_recv.at[d, h, s], sibling
+        )
+
+    own = [pltpu.make_async_copy(x_ref.at[h], all_ref.at[me, h], own_sem.at[h]) for h in range(2)]
+    own.append(pltpu.make_async_copy(looked_ref.at[me], got_ref.at[me], own_sem.at[2]))
+    greet_all(me, n)
+    for d, h in streams:
+        ring(d, h, 0).start()
+
+    def send_looked(peer):
+        push(
+            looked_ref.at[peer], got_ref.at[me], got_send.at[peer], got_recv.at[me], peer
+        ).start()
+
+    each_peer(me, n, send_looked)
+    ends = [q_ref.at[pl.ds(0, BLOCK)], q_ref.at[pl.ds(row_count - BLOCK, BLOCK)]]
+    holders = [0, n - 1]
+
+    def send_end(e, peer):
+        return push(
+            ends[e], ends_ref.at[e], ends_send.at[e, peer], ends_recv.at[e], peer
+        )
+
+    for e in range(2):
+
+        @pl.when(me == holders[e])
+        def _():
+            each_peer(me, n, lambda peer: send_end(e, peer).start())
+            copy = pltpu.make_async_copy(ends[e], ends_ref.at[e], own_sem.at[3])
+            copy.start()
+            copy.wait()
+
+    for copy in own:
+        copy.start()
+    for h in range(2):
+        side(0, h, 0, core).start()
+    for s in range(half):
+        for d, h in streams:
+            if s < hops(d, h):
+                arrival(d, h, s).wait_recv()
+                if s + 1 < hops(d, h):
+                    ring(d, h, s + 1).start()
+                side(d, h, s + 1, core).start()
+    for h in range(2):
+        side(0, h, 0, core).wait_send()
+        side(0, h, 0, 1 - core).wait_recv()
+    for s in range(half):
+        for d, h in streams:
+            if s < hops(d, h):
+                ring(d, h, s).wait_send()
+                side(d, h, s + 1, core).wait_send()
+                side(d, h, s + 1, 1 - core).wait_recv()
+
+    def end_looked(peer):
+        copy = push(
+            looked_ref.at[peer], got_ref.at[peer], got_send.at[peer], got_recv.at[peer], peer
+        )
+        copy.wait_recv()
+        copy.wait_send()
+
+    each_peer(me, n, end_looked)
+    for e in range(2):
+
+        @pl.when(me == holders[e])
+        def _():
+            each_peer(me, n, lambda peer: send_end(e, peer).wait_send())
+
+        @pl.when(me != holders[e])
+        def _():
+            send_end(e, sibling).wait_recv()
+
+    for copy in own:
+        copy.wait()
+
+
+def gather_inputs(x, q, looked):
+    n = lax.axis_size("ctx")
+    rows, features = x.shape
+    half = n // 4
+    dma = pltpu.SemaphoreType.DMA
+    gathered, ends, got = pl.pallas_call(
+        functools.partial(gather_kernel, n),
+        out_shape=[
+            jax.ShapeDtypeStruct((n, 2, rows // 2, features), x.dtype),
+            jax.ShapeDtypeStruct((2, BLOCK, features), q.dtype),
+            jax.ShapeDtypeStruct(looked.shape, looked.dtype),
+        ],
+        in_specs=[ANY] * 3,
+        out_specs=[ANY] * 3,
+        scratch_shapes=[
+            dma((2, 2, half)),
+            dma((2, 2, half)),
+            dma((2, 2, half + 1)),
+            dma((2, 2, half + 1)),
+            dma((n,)),
+            dma((n,)),
+            dma((2, n)),
+            dma((2,)),
+            dma((4,)),
+        ],
+        compiler_params=pltpu.CompilerParams(collective_id=1, has_side_effects=True),
+        name="gather_inputs",
+    )(x.reshape(2, rows // 2, features), q, looked)
+    return gathered.reshape(n * rows // BLOCK, BLOCK, features), ends, got
+
+
+def ends_kernel(
+    n,
+    mine_ref,
+    out_ref,
+    log_ref,
+    rows_ref,
+    outs_ref,
+    logs_ref,
+    rows_send,
+    rows_recv,
+    ends_send,
+    ends_recv,
+    own_sem,
+):
+    me = lax.axis_index("ctx")
+    holders = [0, n - 1]
+    pairs = [(out_ref, outs_ref), (log_ref, logs_ref)]
+
+    def end(e, i, slot):
+        source, target = pairs[i]
+        return push(
+            source.at[e], target.at[slot], ends_send.at[e, i], ends_recv.at[i, slot], holders[e]
+        )
+
+    own = pltpu.make_async_copy(mine_ref, rows_ref.at[me], own_sem.at[2])
+    own.start()
+    greet_all(me, n)
+    for e in range(2):
+
+        @pl.when(me != holders[e])
+        def _():
+            for i in range(2):
+                end(e, i, me).start()
+
+        @pl.when(me == holders[e])
+        def _():
+            for i in range(2):
+                source, target = pairs[i]
+                copy = pltpu.make_async_copy(source.at[e], target.at[me], own_sem.at[i])
+                copy.start()
+                copy.wait()
+
+    def send_rows(peer):
+        push(mine_ref, rows_ref.at[me], rows_send.at[peer], rows_recv.at[me], peer).start()
+
+    each_peer(me, n, send_rows)
+
+    def end_rows(peer):
+        copy = push(mine_ref, rows_ref.at[peer], rows_send.at[peer], rows_recv.at[peer], peer)
+        copy.wait_recv()
+        copy.wait_send()
+
+    each_peer(me, n, end_rows)
+    for e in range(2):
+
+        @pl.when(me != holders[e])
+        def _():
+            for i in range(2):
+                end(e, i, me).wait_send()
+
+        @pl.when(me == holders[e])
+        def _():
+            def arrived(peer):
+                for i in range(2):
+                    source, target = pairs[i]
+                    push(
+                        source.at[e],
+                        target.at[peer],
+                        ends_send.at[e, i],
+                        ends_recv.at[i, peer],
+                        peer,
+                    ).wait_recv()
+
+            each_peer(me, n, arrived)
+
+    own.wait()
+
+
+def send_ends(mine, out, log):
+    n = lax.axis_size("ctx")
+    dma = pltpu.SemaphoreType.DMA
+    out = out.reshape(2, BLOCK, out.shape[1])
+    log = log.reshape(2, BLOCK, LANES)
+    return pl.pallas_call(
+        functools.partial(ends_kernel, n),
+        out_shape=[
+            jax.ShapeDtypeStruct((n,) + mine.shape, mine.dtype),
+            jax.ShapeDtypeStruct((n,) + out.shape[1:], out.dtype),
+            jax.ShapeDtypeStruct((n,) + log.shape[1:], log.dtype),
+        ],
+        in_specs=[ANY] * 3,
+        out_specs=[ANY] * 3,
+        scratch_shapes=[dma((n,)), dma((n,)), dma((2, 2)), dma((2, n)), dma((3,))],
+        compiler_params=pltpu.CompilerParams(collective_id=2, has_side_effects=True),
+        name="send_ends",
+    )(mine, out, log)
+
+
+def combine(outs_ref, logs_ref, total_ref):
+    n, rows, features = outs_ref.shape
+    peak = lax.fori_loop(
+        1, n, lambda i, peak: jnp.maximum(peak, logs_ref[i]), logs_ref[0]
+    )
+    left = lax.broadcasted_iota(jnp.int32, (rows, LANES), 1) < HEAD
+    total_ref[...] = jnp.zeros_like(total_ref)
+
+    def spread(x, p):
+        return jnp.where(left, x[:, 2 * p : 2 * p + 1], x[:, 2 * p + 1 : 2 * p + 2])
+
+    def add(i, total):
+        weights = jnp.exp(logs_ref[i] - peak)
+        for p in range(PAIRS):
+            lanes = slice(p * LANES, (p + 1) * LANES)
+            total_ref[:, lanes] += outs_ref[i, :, lanes].astype(jnp.float32) * spread(weights, p)
+        return total + weights
+
+    scale = 1.0 / lax.fori_loop(0, n, add, jnp.zeros((rows, LANES), jnp.float32))
+    for p in range(PAIRS):
+        lanes = slice(p * LANES, (p + 1) * LANES)
+        total_ref[:, lanes] = total_ref[:, lanes] * spread(scale, p)
+
+
+def summary_kernel(
+    n,
+    part_ref,
+    log_ref,
+    out_ref,
+    outs_ref,
+    logs_ref,
+    total_ref,
+    send_sem,
+    recv_sem,
+    own_sem,
+):
+    me = lax.axis_index("ctx")
+    pairs = [(part_ref, outs_ref), (log_ref, logs_ref)]
     own = [
-        pltpu.make_async_copy(piece(sources[i], me), targets[i].at[me], own_sem.at[i])
-        for i in range(count)
+        pltpu.make_async_copy(source.at[me], target.at[me], own_sem.at[i])
+        for i, (source, target) in enumerate(pairs)
     ]
     for copy in own:
         copy.start()
-    pl.semaphore_wait(barrier, n - 1)
-
-    def push(i, peer, slot):
-        return pltpu.make_async_remote_copy(
-            piece(sources[i], peer),
-            targets[i].at[slot],
-            send_sem.at[i, peer],
-            recv_sem.at[i, slot],
-            device_id={"ctx": peer},
-            device_id_type=MESH,
-        )
-
-    def send(k, carry):
-        peer = lax.rem(me + k, n)
-        for i in range(count):
-            push(i, peer, me).start()
-        return carry
-
-    lax.fori_loop(1, n, send, 0)
-
-    def finish(k, carry):
-        peer = lax.rem(me + n - k, n)
-        for i in range(count):
-            push(i, peer, peer).wait_recv()
-            push(i, peer, peer).wait_send()
-        return carry
-
-    lax.fori_loop(1, n, finish, 0)
+    greet_all(me, n)
+
+    def copies(peer, slot):
+        return [
+            push(
+                source.at[peer], target.at[slot], send_sem.at[i, peer], recv_sem.at[i, slot], peer
+            )
+            for i, (source, target) in enumerate(pairs)
+        ]
+
+    def send(peer):
+        for copy in copies(peer, me):
+            copy.start()
+
+    each_peer(me, n, send)
+
+    def finish(peer):
+        for copy in copies(peer, peer):
+            copy.wait_recv()
+            copy.wait_send()
+
+    each_peer(me, n, finish)
     for copy in own:
         copy.wait()
-
-
-def exchange(arrays, collective_id, same=False):
-    n = lax.axis_size("ctx")
-    count = len(arrays)
-    shapes = [((n,) + x.shape) if same else x.shape for x in arrays]
+    combine(outs_ref, logs_ref, total_ref)
+    out_ref[...] = total_ref[...].astype(out_ref.dtype)
+
+
+def combined_summary(part, logs):
+    n, share, features = part.shape
+    dma = pltpu.SemaphoreType.DMA
     return pl.pallas_call(
-        functools.partial(exchange_kernel, n, count, same),
-        out_shape=[jax.ShapeDtypeStruct(s, x.dtype) for s, x in zip(shapes, arrays)],
-        in_specs=[ANY] * count,
-        out_specs=[ANY] * count,
+        functools.partial(summary_kernel, n),
+        out_shape=jax.ShapeDtypeStruct((share, features), jnp.bfloat16),
+        in_specs=[ANY] * 2,
+        out_specs=VMEM,
         scratch_shapes=[
-            pltpu.SemaphoreType.DMA((count, n)),
-            pltpu.SemaphoreType.DMA((count, n)),
-            pltpu.SemaphoreType.DMA((count,)),
+            pltpu.VMEM(part.shape, part.dtype),
+            pltpu.VMEM(logs.shape, logs.dtype),
+            pltpu.VMEM((share, features), jnp.float32),
+            dma((2, n)),
+            dma((2, n)),
+            dma((2,)),
         ],
-        compiler_params=pltpu.CompilerParams(collective_id=collective_id, has_side_effects=True),
-        name=f"exchange_{collective_id}",
-    )(*arrays)
+        compiler_params=pltpu.CompilerParams(collective_id=3, has_side_effects=True),
+        name="combined_summary",
+    )(part, logs)
 
 
 def dot_t(a, b):
@@ -181,13 +491,15 @@
     x_ref,
     w_kv_ref,
     w_cross_ref,
-    ends_ref,
+    outs_ref,
+    logs_ref,
     sq_ref,
     attended_ref,
     out_ref,
     log_ref,
     rows_ref,
     kv_ref,
+    total_ref,
     sem,
 ):
     row_count, features = x_ref.shape
@@ -245,13 +557,17 @@
 
     lax.fori_loop(0, block_count, one_block, 0)
 
+    def place(rows):
+        combine(outs_ref, logs_ref, total_ref)
+        attended_ref[rows] = total_ref[...].astype(jnp.bfloat16)
+
     @pl.when(edge_ref[0] == 0)
     def _():
-        attended_ref[:BLOCK] = ends_ref[:BLOCK]
+        place(slice(0, BLOCK))
 
     @pl.when(edge_ref[0] + block_count == edge_ref[1])
     def _():
-        attended_ref[row_count - BLOCK :] = ends_ref[BLOCK:]
+        place(slice(row_count - BLOCK, row_count))
 
     encoded = x_ref[...].astype(jnp.float32) + attended_ref[...].astype(jnp.float32)
     rows_ref[:row_count] = encoded.astype(jnp.bfloat16)
@@ -259,7 +575,7 @@
     partial_attention(sq_ref, kv_ref.at[:row_count], out_ref, log_ref)
 
 
-def block_attention(ids, edge, everything, q, x, w_kv, w_cross, ends, sq, pick_count):
+def block_attention(ids, edge, everything, q, x, w_kv, w_cross, outs, end_logs, sq, pick_count):
     slots = ids.shape[0]
     features = x.shape[1]
     return pl.pallas_call(
@@ -269,11 +585,12 @@
             jax.ShapeDtypeStruct(sq.shape, jnp.bfloat16),
             jax.ShapeDtypeStruct((sq.shape[0], LANES), jnp.float32),
         ],
-        in_specs=[SMEM, SMEM, ANY] + [VMEM] * 6,
+        in_specs=[SMEM, SMEM, ANY] + [VMEM] * 7,
         out_specs=[VMEM] * 3,
         scratch_shapes=[
             pltpu.VMEM((slots * BLOCK, features), jnp.bfloat16),
             pltpu.VMEM((slots * BLOCK, 2 * features), jnp.bfloat16),
+            pltpu.VMEM((BLOCK, features), jnp.float32),
             pltpu.SemaphoreType.DMA((slots,)),
         ],
         compiler_params=pltpu.CompilerParams(vmem_limit_bytes=VMEM_LIMIT),
@@ -281,22 +598,7 @@
             flops=20 << 30, bytes_accessed=16 << 20, transcendentals=5 << 20
         ),
         name="block_attention",
-    )(ids, edge, everything, q, x, w_kv, w_cross, ends, sq)
-
-
-def combined(outs, logs):
-    n, rows, features = outs.shape
-    logs = logs[:, :, :HEADS]
-    weights = jnp.exp(logs - jnp.max(logs, axis=0, keepdims=True))
-    weights = weights / jnp.sum(weights, axis=0, keepdims=True)
-    spread = jnp.broadcast_to(weights[:, :, :, None], (n, rows, HEADS, HEAD))
-    spread = spread.reshape(n, rows, features)
-    return jnp.sum(outs.astype(jnp.float32) * spread, axis=0).astype(jnp.bfloat16)
-
-
-def dealt(x, n, each):
-    x = jnp.pad(x, ((0, n * each - x.shape[0]), (0, 0)))
-    return x.reshape(n, each, x.shape[1])
+    )(ids, edge, everything, q, x, w_kv, w_cross, outs, end_logs, sq)
 
 
 def local(queries, inputs, w_kv, rand_blocks, w_cross, vocab_table, summary_ids):
@@ -309,50 +611,17 @@
     shard_rows = vocab_table.shape[0]
     summary_count = summary_ids.shape[0]
     share = summary_count // n
-    each = -(-BLOCK // n)
-
-    everything = lax.all_gather(inputs, "ctx", axis=0, tiled=True)
-    everything = everything.reshape(total_blocks, BLOCK, features)
-
     offsets = summary_ids - position * shard_rows
     inside = jnp.logical_and(offsets >= 0, offsets < shard_rows)
     looked = vocab_table[jnp.clip(offsets, 0, shard_rows - 1)]
     looked = jnp.where(inside[:, None], looked, jnp.zeros((), looked.dtype))
-    message = jnp.concatenate(
-        [
-            looked.reshape(n, share, features),
-            dealt(queries[:BLOCK], n, each),
-            dealt(queries[row_count - BLOCK :], n, each),
-        ],
-        axis=1,
+    everything, end_queries, got = gather_inputs(
+        inputs, queries, looked.reshape(n, share, features)
     )
-    (received,) = exchange([message], 1)
-    mine = jnp.concatenate(
-        [
-            jnp.sum(received[:, :share].astype(jnp.float32), axis=0).astype(jnp.bfloat16),
-            received[0, share : share + each],
-            received[n - 1, share + each :],
-        ],
-        axis=0,
-    )
-    (rows,) = exchange([mine], 2, same=True)
-    summary_queries = rows[:, :share].reshape(summary_count, features)
-    first = rows[:, share : share + each].reshape(n * each, features)[:BLOCK]
-    last = rows[:, share + each :].reshape(n * each, features)[:BLOCK]
-    end_out, end_log = global_partial(jnp.concatenate([first, last], axis=0), inputs, w_kv)
-
-    def split(x):
-        return jnp.concatenate([dealt(x[:BLOCK], n, each), dealt(x[BLOCK:], n, each)], axis=1)
-
-    got_out, got_log = exchange([split(end_out), split(end_log)], 3)
-    (ends,) = exchange([combined(got_out, got_log)], 4, same=True)
-    ends = jnp.concatenate(
-        [
-            ends[:, :each].reshape(n * each, features)[:BLOCK],
-            ends[:, each:].reshape(n * each, features)[:BLOCK],
-        ],
-        axis=0,
-    )
+    mine = jnp.sum(got.astype(jnp.float32), axis=0).astype(jnp.bfloat16)
+    end_out, end_log = global_partial(end_queries.reshape(2 * BLOCK, features), inputs, w_kv)
+    rows, outs, end_logs = send_ends(mine, end_out, end_log)
+    summary_queries = rows.reshape(summary_count, features)
 
     start = position * block_count
     near = jnp.clip(start - 1 + jnp.arange(block_count + 2, dtype=jnp.int32), 0, total_blocks - 1)
@@ -361,12 +630,22 @@
     ids = jnp.concatenate([near, fixed, picks.astype(jnp.int32)])
     edge = jnp.stack([start, jnp.full_like(start, total_blocks)]).astype(jnp.int32)
     attended, part, logs = block_attention(
-        ids, edge, everything, queries, inputs, w_kv, w_cross, ends, summary_queries, pick_count
+        ids,
+        edge,
+        everything,
+        queries,
+        inputs,
+        w_kv,
+        w_cross,
+        outs,
+        end_logs,
+        summary_queries,
+        pick_count,
     )
-    parts, all_logs = exchange(
-        [part.reshape(n, share, features), logs.reshape(n, share, LANES)], 5
+    summary = combined_summary(
+        part.reshape(n, share, features), logs.reshape(n, share, LANES)
     )
-    return attended, combined(parts, all_logs)
+    return attended, summary
 
 
 def solution(mesh):

time: 220 us -> 209 us (0.950)
  Pallas kernels: 169 us -> 190 us
  between operations: 14.3 us -> 0.75 us
  other arithmetic: 14.5 us -> 4.26 us
  waiting for transfers between devices: 6.77 us -> 0 us
    pallas_call x5 -> x3, Pallas kernels: 125 us -> 146 us  [the longest x1 90 us: gather_inputs(): pl.pallas_call(functools.partial(gather_kernel, n), out_shape=[jax.ShapeD...]
    unnamed x20 -> x25, local copies, waits for them, and re-layouts: 3.65 us -> 10.9 us
    all_gather x1 -> x0, waiting for transfers between devices: 6.08 us -> none  [local(): everything = lax.all_gather(inputs, 'ctx', axis=0, tiled=True)]
    reduce_sum x5 -> x1, other arithmetic: 6.7 us -> 1.75 us  [local(): mine = jnp.sum(got.astype(jnp.float32), axis=0).astype(jnp.bfloat16)]
    slice x6 -> x0, local copies, waits for them, and re-layouts: 4.64 us -> none  [the longest x1 1.3 us: local(): first = rows[:, share:share + each].reshape(n * each, features)[:BLOCK]]
    concatenate x6 -> x0, other arithmetic: 3.18 us -> none  [the longest x2 1.48 us: split(): jnp.concatenate([dealt(x[:BLOCK], n, each), dealt(x[BLOCK:], n, each)], a...]
    reshape x10 -> x0, local copies, waits for them, and re-layouts: 3.02 us -> none  [the longest x2 2.64 us: combined(): spread = spread.reshape(n, rows, features)]
  transfers between devices with their start and end apart: 1 -> 0, of which waited for: 1 -> 0; matrix products, arithmetic and copies ran while one was open for 8% -> 0% of each run, Pallas kernels for 49% -> 0%
where the time goes in v2:
time: 209 us; the launch traced here: 208 us
  Pallas kernels  190 us (91%)
  local copies, waits for them, and re-layouts  13.1 us (6%)
  other arithmetic  4.26 us (2%)
    pallas_call x1, Pallas kernels, gather_inputs(): pl.pallas_call(functools.partial(gather_kernel, n), out_shape=[jax.ShapeD...  90 us
    pallas_call x1, Pallas kernels, block_attention(): pl.pallas_call(functools.partial(block_kernel, pick_count), out_shape=[ja...  39 us
    pallas_call x1, Pallas kernels, send_ends(): pl.pallas_call(functools.partial(ends_kernel, n), out_shape=[jax.ShapeDty...  29.6 us
    pallas_call x1, Pallas kernels, combined_summary(): pl.pallas_call(functools.partial(summary_kernel, n), out_shape=jax.ShapeD...  26.6 us
    unnamed x25, local copies, waits for them, and re-layouts  10.9 us
    pallas_call x1, Pallas kernels, global_partial(): pl.pallas_call(global_kernel, out_shape=[jax.ShapeDtypeStruct(q.shape, jn...  4.7 us

profile of v2, /device:TPU:11, one launch (start us, length us, event | category | flops | bytes accessed | tf_op | source)
XLA Modules:
  0.0 208.1 jit_solution(1932091209860315420)
XLA Ops:
  0.7 0.8 compare_and_fusion
  1.4 0.7 compare_select_fusion
  2.2 0.1 broadcast_in_dim.18
  2.3 0.8 constant_dynamic-slice_fusion
  3.0 0.1 copy.11
  3.1 0.1 reshape.39
  3.3 1.2 gather_fusion
  4.5 0.9 broadcast_select_fusion.looked_ref
  5.4 90.0 %gather_inputs.1 = (bf16[16,2,192,1024]{3,2,1,0:T(8,128)(2,1)}, bf16[2,64,1024]{2,1,0:T(8,128)(2,1)}, bf16[16,16,1024]{2,1,0:T(8,128)(2,1)}) custom-call(bf16[2,192,1024]{2,1,0:T(8,128)(2,1)} %bitcast.10, bf16[384,1024]{1,0:T(8,128)(2,1)} %q_ref.3, bf16[16,16,1024]{2,1,0:T(8,128)(2,1)} %broadcast_select_fusion.looked_ref), custom_call_target="tpu_custom_call" | custom-call | tf_op jit(solution)/shard_map/gather_inputs/pallas_call | solution.py:190
  95.4 1.7 reduce_sum.12.mine_ref
  97.2 2.2 %copy-done.7 = bf16[1024,2048]{1,0:T(8,128)(2,1)S(1)} copy-done((bf16[1024,2048]{1,0:T(8,128)(2,1)S(1)}, bf16[1024,2048]{1,0:T(8,128)(2,1)}, u32[]{:S(2)}) %copy-start.7) | copy-done | bytes 4194328
  99.4 0.9 copy-done.11
  100.3 4.7 %global_partial.1 = (bf16[128,1024]{1,0:T(8,128)(2,1)S(1)}, f32[128,128]{1,0:T(8,128)S(1)}) custom-call(bf16[128,1024]{1,0:T(8,128)(2,1)S(1)} %bitcast.16, bf16[384,1024]{1,0:T(8,128)(2,1)S(1)} %copy-done.1, bf16[1024,2048]{1,0:T(8,128)(2,1)S(1)} %copy-done.7), custom_call_target="tpu_custom_call" | custom-call | flops 1610612736 | bytes 6291456 | tf_op jit(solution)/shard_map/global_partial/pallas_call | solution.py:468
  105.0 0.7 copy-done.4
  105.7 0.6 copy-done.6
  106.3 29.6 %send_ends.1 = (bf16[16,16,1024]{2,1,0:T(8,128)(2,1)}, bf16[16,64,1024]{2,1,0:T(8,128)(2,1)}, f32[16,64,128]{2,1,0:T(8,128)}) custom-call(bf16[16,1024]{1,0:T(8,128)(2,1)} %reduce_sum.12.mine_ref, bf16[2,64,1024]{2,1,0:T(8,128)(2,1)} %bitcast.12, f32[2,64,128]{2,1,0:T(8,128)} %bitcast.14), custom_call_target="tpu_custom_call" | custom-call | tf_op jit(solution)/shard_map/send_ends/pallas_call | solution.py:299
  136.0 1.6 copy-done.8
  137.5 1.0 copy-done.9
  138.6 1.0 copy-done.10
  139.6 39.0 %block_attention.1 = (bf16[384,1024]{1,0:T(8,128)(2,1)}, bf16[256,1024]{1,0:T(8,128)(2,1)S(1)}, f32[256,128]{1,0:T(8,128)S(1)}) custom-call(s32[28]{0:T(128)S(1)} %pad_add_fusion.ids_ref, s32[2]{0:T(128)S(1)} %pad_add_fusion.1.edge_ref, bf16[96,64,1024]{2,1,0:T(8,128)(2,1)} %bitcast.18, bf16[384,1024]{1,0:T(8,128)(2,1)S(1)} %copy-done.2, ...), custom_call_target="tpu_custom_call" | custom-call | flops 21474836480 | bytes 16777216 | tf_op jit(solution)/shard_map/block_attention/pallas_call | solution.py:581
  178.7 0.8 copy-done.3
  179.5 0.6 copy-done.5
  180.1 26.6 %combined_summary.1 = bf16[16,1024]{1,0:T(8,128)(2,1)} custom-call(bf16[16,16,1024]{2,1,0:T(8,128)(2,1)} %bitcast.11, f32[16,16,128]{2,1,0:T(8,128)} %bitcast.13), custom_call_target="tpu_custom_call" | custom-call | tf_op jit(solution)/shard_map/combined_summary/pallas_call | solution.py:389
  206.7 1.4 copy.13
  (20 shorter events, 0.2 us)
Async XLA Ops:
  0.6 2.7 %copy-start = (bf16[384,1024]{1,0:T(8,128)(2,1)S(1)}, bf16[384,1024]{1,0:T(8,128)(2,1)}, u32[]{:S(2)}) copy-start(bf16[384,1024]{1,0:T(8,128)(2,1)} %param.13) | copy-start | bytes 2359300
  3.3 93.9 %copy-start.1 = (bf16[384,1024]{1,0:T(8,128)(2,1)S(1)}, bf16[384,1024]{1,0:T(8,128)(2,1)}, u32[]{:S(2)}) copy-start(bf16[384,1024]{1,0:T(8,128)(2,1)} %x_ref.3) | copy-start | bytes 2359300
  5.4 130.6 %copy-start.2 = (bf16[384,1024]{1,0:T(8,128)(2,1)S(1)}, bf16[384,1024]{1,0:T(8,128)(2,1)}, u32[]{:S(2)}) copy-start(bf16[384,1024]{1,0:T(8,128)(2,1)} %q_ref.3) | copy-start | bytes 2359300
  97.2 2.2 %copy-start.7 = (bf16[1024,2048]{1,0:T(8,128)(2,1)S(1)}, bf16[1024,2048]{1,0:T(8,128)(2,1)}, u32[]{:S(2)}) copy-start(bf16[1024,2048]{1,0:T(8,128)(2,1)} %w_kv_ref.1) | copy-start | bytes 12582916
  99.4 0.9 copy-start.11
  105.0 0.7 copy-start.4
  105.7 0.6 copy-start.6
  135.9 1.6 copy-start.8
  137.5 1.0 copy-start.9
  138.6 1.0 copy-start.10
  178.7 0.8 copy-start.3
  179.5 0.6 copy-start.5

commit v3 on v2

--- a/solution.py
+++ b/solution.py
@@ -125,19 +125,45 @@
     ends = [q_ref.at[pl.ds(0, BLOCK)], q_ref.at[pl.ds(row_count - BLOCK, BLOCK)]]
     holders = [0, n - 1]
 
-    def send_end(e, peer):
-        return push(
-            ends[e], ends_ref.at[e], ends_send.at[e, peer], ends_recv.at[e], peer
-        )
+    steps = [(place - at + chips) % chips for at in (0, half)]
+    right, left = device(place + 1, core), device(place - 1, core)
+
+    def send_end(e, k, source):
+        peer = (right, left, sibling)[k]
+        return push(source, ends_ref.at[e], ends_send.at[e, k], ends_recv.at[e], peer)
+
+    def routes(e):
+        away = steps[e]
+        return [
+            (0, away < half),
+            (1, jnp.logical_or(away == 0, away > chips - half + 1)),
+            (2, me == holders[e]),
+        ]
+
+    def start_routes(e, source):
+        for k, goes in routes(e)[:2]:
+
+            @pl.when(goes)
+            def _():
+                send_end(e, k, source).start()
+
+    def pass_end(e):
+        send_end(e, 0, ends_ref.at[e]).wait_recv()
+        start_routes(e, ends_ref.at[e])
 
     for e in range(2):
 
         @pl.when(me == holders[e])
         def _():
-            each_peer(me, n, lambda peer: send_end(e, peer).start())
+            send_end(e, 2, ends[e]).start()
+            start_routes(e, ends[e])
             copy = pltpu.make_async_copy(ends[e], ends_ref.at[e], own_sem.at[3])
             copy.start()
             copy.wait()
+
+        @pl.when(jnp.logical_and(steps[e] == 0, me != holders[e]))
+        def _():
+            pass_end(e)
 
     for copy in own:
         copy.start()
@@ -150,6 +176,15 @@
                 if s + 1 < hops(d, h):
                     ring(d, h, s + 1).start()
                 side(d, h, s + 1, core).start()
+        for e in range(2):
+            near = steps[e] == s + 1
+            if s + 1 < half:
+                near = jnp.logical_or(near, steps[e] == chips - s - 1)
+
+            @pl.when(near)
+            def _():
+                pass_end(e)
+
     for h in range(2):
         side(0, h, 0, core).wait_send()
         side(0, h, 0, 1 - core).wait_recv()
@@ -169,14 +204,11 @@
 
     each_peer(me, n, end_looked)
     for e in range(2):
-
-        @pl.when(me == holders[e])
-        def _():
-            each_peer(me, n, lambda peer: send_end(e, peer).wait_send())
-
-        @pl.when(me != holders[e])
-        def _():
-            send_end(e, sibling).wait_recv()
+        for k, goes in routes(e):
+
+            @pl.when(goes)
+            def _():
+                send_end(e, k, ends[e]).wait_send()
 
     for copy in own:
         copy.wait()
@@ -203,7 +235,7 @@
             dma((2, 2, half + 1)),
             dma((n,)),
             dma((n,)),
-            dma((2, n)),
+            dma((2, 3)),
             dma((2,)),
             dma((4,)),
         ],

time: 209 us -> 195 us (0.933)
  Pallas kernels: 190 us -> 176 us
    pallas_call x1, Pallas kernels: 90 us -> 81.6 us  [gather_inputs(): pl.pallas_call(functools.partial(gather_kernel, n), out_shape=[jax.ShapeD...]
    pallas_call x1, Pallas kernels: 29.6 us -> 24.6 us  [send_ends(): pl.pallas_call(functools.partial(ends_kernel, n), out_shape=[jax.ShapeDty...]
where the time goes in v3:
time: 195 us
  Pallas kernels  176 us (90%)
  local copies, waits for them, and re-layouts  13.1 us (7%)
  other arithmetic  4.26 us (2%)
    pallas_call x1, Pallas kernels, gather_inputs(): pl.pallas_call(functools.partial(gather_kernel, n), out_shape=[jax.ShapeD...  81.6 us
    pallas_call x1, Pallas kernels, block_attention(): pl.pallas_call(functools.partial(block_kernel, pick_count), out_shape=[ja...  39 us
    pallas_call x1, Pallas kernels, combined_summary(): pl.pallas_call(functools.partial(summary_kernel, n), out_shape=jax.ShapeD...  26.6 us
    pallas_call x1, Pallas kernels, send_ends(): pl.pallas_call(functools.partial(ends_kernel, n), out_shape=[jax.ShapeDty...  24.6 us
    unnamed x25, local copies, waits for them, and re-layouts  10.9 us
    pallas_call x1, Pallas kernels, global_partial(): pl.pallas_call(global_kernel, out_shape=[jax.ShapeDtypeStruct(q.shape, jn...  4.69 us

profile of v3, /device:TPU:11, one launch (start us, length us, event | category | flops | bytes accessed | tf_op | source)
XLA Modules:
  0.0 194.6 jit_solution(2761259130612361834)
XLA Ops:
  0.7 0.8 compare_and_fusion
  1.4 0.7 compare_select_fusion
  2.2 0.1 broadcast_in_dim.18
  2.3 0.8 constant_dynamic-slice_fusion
  3.0 0.1 copy.11
  3.1 0.1 reshape.39
  3.3 1.2 gather_fusion
  4.5 0.9 broadcast_select_fusion.looked_ref
  5.4 81.6 %gather_inputs.1 = (bf16[16,2,192,1024]{3,2,1,0:T(8,128)(2,1)}, bf16[2,64,1024]{2,1,0:T(8,128)(2,1)}, bf16[16,16,1024]{2,1,0:T(8,128)(2,1)}) custom-call(bf16[2,192,1024]{2,1,0:T(8,128)(2,1)} %bitcast.10, bf16[384,1024]{1,0:T(8,128)(2,1)} %q_ref.3, bf16[16,16,1024]{2,1,0:T(8,128)(2,1)} %broadcast_select_fusion.looked_ref), custom_call_target="tpu_custom_call" | custom-call | tf_op jit(solution)/shard_map/gather_inputs/pallas_call | solution.py:222
  86.9 1.7 reduce_sum.12.mine_ref
  88.7 2.2 %copy-done.7 = bf16[1024,2048]{1,0:T(8,128)(2,1)S(1)} copy-done((bf16[1024,2048]{1,0:T(8,128)(2,1)S(1)}, bf16[1024,2048]{1,0:T(8,128)(2,1)}, u32[]{:S(2)}) %copy-start.7) | copy-done | bytes 4194328
  90.9 0.9 copy-done.11
  91.8 4.7 %global_partial.1 = (bf16[128,1024]{1,0:T(8,128)(2,1)S(1)}, f32[128,128]{1,0:T(8,128)S(1)}) custom-call(bf16[128,1024]{1,0:T(8,128)(2,1)S(1)} %bitcast.16, bf16[384,1024]{1,0:T(8,128)(2,1)S(1)} %copy-done.1, bf16[1024,2048]{1,0:T(8,128)(2,1)S(1)} %copy-done.7), custom_call_target="tpu_custom_call" | custom-call | flops 1610612736 | bytes 6291456 | tf_op jit(solution)/shard_map/global_partial/pallas_call | solution.py:500
  96.5 0.7 copy-done.4
  97.2 0.6 copy-done.6
  97.9 24.6 %send_ends.1 = (bf16[16,16,1024]{2,1,0:T(8,128)(2,1)}, bf16[16,64,1024]{2,1,0:T(8,128)(2,1)}, f32[16,64,128]{2,1,0:T(8,128)}) custom-call(bf16[16,1024]{1,0:T(8,128)(2,1)} %reduce_sum.12.mine_ref, bf16[2,64,1024]{2,1,0:T(8,128)(2,1)} %bitcast.12, f32[2,64,128]{2,1,0:T(8,128)} %bitcast.14), custom_call_target="tpu_custom_call" | custom-call | tf_op jit(solution)/shard_map/send_ends/pallas_call | solution.py:331
  122.4 1.6 copy-done.8
  124.0 1.0 copy-done.9
  125.1 1.0 copy-done.10
  126.1 39.0 %block_attention.1 = (bf16[384,1024]{1,0:T(8,128)(2,1)}, bf16[256,1024]{1,0:T(8,128)(2,1)S(1)}, f32[256,128]{1,0:T(8,128)S(1)}) custom-call(s32[28]{0:T(128)S(1)} %pad_add_fusion.ids_ref, s32[2]{0:T(128)S(1)} %pad_add_fusion.1.edge_ref, bf16[96,64,1024]{2,1,0:T(8,128)(2,1)} %bitcast.18, bf16[384,1024]{1,0:T(8,128)(2,1)S(1)} %copy-done.2, ...), custom_call_target="tpu_custom_call" | custom-call | flops 21474836480 | bytes 16777216 | tf_op jit(solution)/shard_map/block_attention/pallas_call | solution.py:613
  165.2 0.8 copy-done.3
  165.9 0.6 copy-done.5
  166.6 26.6 %combined_summary.1 = bf16[16,1024]{1,0:T(8,128)(2,1)} custom-call(bf16[16,16,1024]{2,1,0:T(8,128)(2,1)} %bitcast.11, f32[16,16,128]{2,1,0:T(8,128)} %bitcast.13), custom_call_target="tpu_custom_call" | custom-call | tf_op jit(solution)/shard_map/combined_summary/pallas_call | solution.py:421
  193.2 1.4 copy.13
  (20 shorter events, 0.2 us)
Async XLA Ops:
  0.6 2.7 %copy-start = (bf16[384,1024]{1,0:T(8,128)(2,1)S(1)}, bf16[384,1024]{1,0:T(8,128)(2,1)}, u32[]{:S(2)}) copy-start(bf16[384,1024]{1,0:T(8,128)(2,1)} %param.13) | copy-start | bytes 2359300
  3.3 85.4 %copy-start.1 = (bf16[384,1024]{1,0:T(8,128)(2,1)S(1)}, bf16[384,1024]{1,0:T(8,128)(2,1)}, u32[]{:S(2)}) copy-start(bf16[384,1024]{1,0:T(8,128)(2,1)} %x_ref.3) | copy-start | bytes 2359300
  5.4 117.0 %copy-start.2 = (bf16[384,1024]{1,0:T(8,128)(2,1)S(1)}, bf16[384,1024]{1,0:T(8,128)(2,1)}, u32[]{:S(2)}) copy-start(bf16[384,1024]{1,0:T(8,128)(2,1)} %q_ref.3) | copy-start | bytes 2359300
  88.7 2.2 %copy-start.7 = (bf16[1024,2048]{1,0:T(8,128)(2,1)S(1)}, bf16[1024,2048]{1,0:T(8,128)(2,1)}, u32[]{:S(2)}) copy-start(bf16[1024,2048]{1,0:T(8,128)(2,1)} %w_kv_ref.1) | copy-start | bytes 12582916
  90.9 0.9 copy-start.11
  96.5 0.7 copy-start.4
  97.2 0.6 copy-start.6
  122.4 1.6 copy-start.8
  124.0 1.0 copy-start.9
  125.1 1.0 copy-start.10
  165.1 0.8 copy-start.3
  165.9 0.6 copy-start.5
